TPU v7x, 32 devices: a whole 2x2x4 slice. The times are simulated.
32 devices in a mesh: row: 4 (over z), col: 8 (over y, x, core).
Axes of the slice: x: 2, y: 2, z: 4, core: 2. Of those that a mesh axis runs over, the one named last changes fastest.
Arguments:
- amplitudes: bfloat16 [16, 16, 12, 4096], P('row', 'col'), may hold values from -6 to 6
- integrals: bfloat16 [16, 16, 47, 4096], P('row', 'col'), may hold values from -0.1875 to 0.1875
- pair_lists: int32 [4, 12, 2], replicated, may hold values from 0 to 46, as said below
- tile_counts: int32 [4], replicated, may hold values from 1 to 12, as said below
Outputs:
- symmetric: float32 [16, 16, 12, 4096], P('row', 'col')
Inputs may be any that keep to these rules, and one draw needn't show every extreme that they name: `pair_lists`: each grid row lists 12 distinct ordered pairs of different tiles. `tile_counts`: the largest count equals 12.
All inputs are finite; a program needn't handle non-finite values.
Results may differ from a plain program's by a relative error of at most 0.0029.
Values may be sent and summed in bfloat16 or wider, within the bound.
No kernel may reach another device: no remote copies, remote signals or barrier semaphores. Data moves between devices by JAX's collectives and lax.ppermute only.
A program may use at most 128 MiB of HBM per device.

v0:
```python
import jax
import jax.numpy as jnp
from jax import lax
from jax.sharding import PartitionSpec as P

TILE = 64


def mirror_pairs(row_devices, col_devices, step):
    ratio = col_devices // row_devices
    pairs = []
    for row in range(row_devices):
        for col in range(col_devices):
            part = (col % ratio + step) % ratio
            pairs.append((row * col_devices + col, col // ratio * col_devices + row * ratio + part))
    return pairs


def on_device(amplitudes, integrals, pair_lists, tile_counts):
    occ_row, occ_col, slot_count, square = amplitudes.shape
    tile_width = TILE
    row_devices = lax.axis_size("row")
    col_devices = lax.axis_size("col")
    col_ratio = col_devices // row_devices
    my_row = lax.axis_index("row")
    my_col = lax.axis_index("col")
    partner_row = my_col // col_ratio
    tile_first = pair_lists[:, :, 0]
    tile_second = pair_lists[:, :, 1]
    packed = jnp.take(integrals, tile_second.reshape(-1), axis=2)
    packed = packed.reshape(occ_row, occ_col, row_devices, slot_count, square)
    received = lax.all_to_all(packed, "row", split_axis=2, concat_axis=0, tiled=True)
    received = received.reshape(occ_row * row_devices, occ_col, slot_count, square)
    piece = lax.all_gather(amplitudes, "col", axis=1, tiled=True)
    piece_count = piece.shape[1]
    left_tiles = piece.reshape(occ_row, piece_count, slot_count, tile_width, tile_width)
    right_tiles = received.reshape(piece_count, occ_col, slot_count, tile_width, tile_width)
    cycle_sum = jnp.einsum(
        "iksac,kjscb->ijsab", left_tiles, right_tiles, preferred_element_type=jnp.float32
    )
    my_count = lax.dynamic_index_in_dim(tile_counts, my_row, 0, keepdims=False)
    live_slots = (jnp.arange(slot_count, dtype=jnp.int32) < my_count).astype(jnp.float32)
    cycle_value = (cycle_sum * live_slots[None, None, :, None, None]).astype(jnp.bfloat16)
    cycle = cycle_value.reshape(occ_row, occ_col, slot_count, square)
    halves = cycle.reshape(col_ratio, occ_col, occ_col, slot_count, square)
    col_part = lax.rem(my_col, col_ratio)
    arrived = []
    for step in range(col_ratio):
        part = lax.rem(col_part + step, col_ratio)
        block = lax.dynamic_index_in_dim(halves, part, 0, keepdims=False)
        arrived.append(
            lax.ppermute(block, ("row", "col"), mirror_pairs(row_devices, col_devices, step))
        )
    arrived = jnp.stack(arrived)
    order = lax.rem(col_part - jnp.arange(col_ratio) + col_ratio, col_ratio)
    arrived = jnp.take(arrived, order, axis=0)
    mirror_block = jnp.moveaxis(arrived, 0, 1).reshape(occ_col, occ_row, slot_count, square)
    mirror_block = mirror_block.reshape(occ_col, occ_row, slot_count, tile_width, tile_width)
    mine_first = lax.dynamic_index_in_dim(tile_first, my_row, 0, keepdims=False)
    mine_second = lax.dynamic_index_in_dim(tile_second, my_row, 0, keepdims=False)
    their_first = lax.dynamic_index_in_dim(tile_first, partner_row, 0, keepdims=False)
    their_second = lax.dynamic_index_in_dim(tile_second, partner_row, 0, keepdims=False)
    pair_match = (
        (mine_first[:, None] == their_second[None, :])
        & (mine_second[:, None] == their_first[None, :])
    ).astype(jnp.bfloat16)
    crossed = jnp.einsum(
        "st,jitba->ijsab", pair_match, mirror_block, preferred_element_type=jnp.float32
    )
    own_part = cycle_value.astype(jnp.float32)
    symmetric = (own_part + crossed) * live_slots[None, None, :, None, None]
    return symmetric.reshape(occ_row, occ_col, slot_count, square)


def solution(mesh):
    return jax.shard_map(
        on_device,
        mesh=mesh,
        in_specs=(P("row", "col", None, None), P("row", "col", None, None), P(), P()),
        out_specs=P("row", "col", None, None),
        check_vma=False,
    )
```

profile of v0, /device:TPU:3, one launch (start us, length us, event | category | flops | bytes accessed | tf_op | source)
XLA Modules:
  0.0 234.9 jit_solution(8737630853103244513)
XLA Ops:
  6.5 0.0 all-gather.2.cloned.1.call-start
  6.5 2.8 %copy.23 = bf16[4,2,12,4096]{3,0,2,1:T(4,128)(2,1)} copy(bf16[4,2,12,4096]{3,1,2,0:T(2,128)(2,1)} %param.4) | data formatting | bytes 1572864 | tf_op args[0]
  9.3 0.0 all-gather.2.cloned.1.call-update
  9.3 0.8 fusion.33
  10.1 0.1 reshape_squeeze.6
  10.2 8.5 %gather_fusion = bf16[48,4,2,4096]{3,2,1,0:T(2,128)(2,1)} fusion(bf16[4,2,47,4096]{3,1,2,0:T(2,128)(2,1)S(1)} %copy-done, s32[1024]{0:T(1024)S(1)} %pad_clamp_fusion.1), kind=kCustom, calls=%fused_computation | custom fusion | bytes 6291648 | tf_op jit(solution)/shard_map/jit(_take)/gather | solution.py:30
  18.7 6.6 %broadcast_select_fusion = bf16[4,2,4,12,4096]{4,1,3,0,2:T(2,128)(2,1)} fusion(pred[4,12]{1,0:T(4,128)(4,1)S(1)} %compare_and_fusion.1, bf16[4,2,4,12,4096]{4,1,0,3,2:T(2,128)(2,1)} %bitcast.73), kind=kLoop, calls=%fused_computation.5 | loop fusion | flops 1572864 | bytes 6291504 | tf_op jit(solution)/shard_map/jit(_take)/select_n | solution.py:30
  25.4 5.0 %all-to-all-start = ((bf16[4,2,4,12,4096]{4,1,3,0,2:T(2,128)(2,1)}), bf16[4,2,4,12,4096]{4,1,3,0,2:T(2,128)(2,1)}, u32[]{:S(2)}, u32[]{:S(2)}) async-start(bf16[4,2,4,12,4096]{4,1,3,0,2:T(2,128)(2,1)} %broadcast_select_fusion), calls=%async_computation | async-start | bytes 6291456 | tf_op jit(solution)/shard_map/all_to_all | solution.py:32
  30.4 0.6 dynamic_slice.24
  31.0 0.6 compare_convert_fusion
  31.7 69.0 %all-to-all-done = bf16[4,2,4,12,4096]{4,1,3,0,2:T(2,128)(2,1)} async-done(((bf16[4,2,4,12,4096]{4,1,3,0,2:T(2,128)(2,1)}), bf16[4,2,4,12,4096]{4,1,3,0,2:T(2,128)(2,1)}, u32[]{:S(2)}, u32[]{:S(2)}) %all-to-all-start) | async-done | bytes 3145760 | tf_op jit(solution)/shard_map/all_to_all | solution.py:32
  100.6 11.1 %reshape_reshape.9 = bf16[16,2,12,64,64]{4,3,1,2,0:T(8,128)(2,1)} reshape(bf16[4,4,2,1,12,4096]{5,2,4,1,0,3:T(2,128)(2,1)} %bitcast.5) | data formatting | bytes 6291456 | tf_op jit(solution)/shard_map/reshape;reshape | solution.py:37
  111.7 9.3 %copy.24 = bf16[4,16,12,4096]{3,1,0,2:T(8,128)(2,1)} copy(bf16[4,16,12,4096]{3,0,2,1:T(4,128)(2,1)} %all-gather.2.cloned.1.call-done) | data formatting | bytes 12582912 | tf_op jit(solution)/shard_map/all_gather | solution.py:34
  121.1 17.9 %reshape.123 = bf16[4,16,12,64,64,1]{4,3,1,0,2,5:T(8,128)(2,1)} reshape(bf16[4,16,12,4096]{3,1,0,2:T(8,128)(2,1)} %copy.24) | data formatting | bytes 12582912 | tf_op jit(solution)/shard_map/reshape | solution.py:36
  139.0 11.1 %fusion.11 = bf16[4,2,12,64,64]{3,4,0,1,2:T(8,128)(2,1)S(1)} fusion(f32[12]{0:T(128)S(1)} %compare_convert_fusion, bf16[4,16,12,64,64,1]{4,3,1,0,2,5:T(8,128)(2,1)} %reshape.123, bf16[16,2,12,64,64]{4,3,1,2,0:T(8,128)(2,1)} %reshape_reshape.9), kind=kOutput, calls=%fused_computation.13 | convolution fusion | flops 806092800 | bytes 10223664 | tf_op jit(solution)/shard_map/iksac,kjscb->ijsab/dot_general | solution.py:38
  150.1 1.7 copy.26
  151.8 3.1 %reshape_reshape.10 = bf16[2,2,2,12,4096]{4,2,3,1,0:T(2,128)(2,1)S(1)} reshape(bf16[4,2,12,64,64]{4,3,1,2,0:T(8,128)(2,1)} %copy.26) | data formatting | bytes 1572864 | tf_op jit(solution)/shard_map/reshape;reshape | solution.py:45
  154.9 0.8 dynamic-slice_bitcast_fusion.1
  155.7 0.1 collective-permute-start.1
  155.8 5.8 %collective-permute-start = (bf16[2,2,12,4096]{3,1,2,0:T(2,128)(2,1)S(1)}, bf16[2,2,12,4096]{3,1,2,0:T(2,128)(2,1)S(1)}, u32[]{:S(2)}, u32[]{:S(2)}) collective-permute-start(bf16[2,2,12,4096]{3,1,2,0:T(2,128)(2,1)S(1)} %get-tuple-element.5), channel_id=1, source_target_pairs={{0,0},{1,1},{2,8},{3,9},{4,16},{5,17},{6,24},{7,25},{8,2},{9,3},{1... | collective-permute-start | bytes 1179656 | tf_op jit(solution)/shard_map/ppermute | solution.py:52
  161.7 39.6 %collective-permute-done.1 = bf16[2,2,12,4096]{3,1,2,0:T(2,128)(2,1)S(1)} collective-permute-done((bf16[2,2,12,4096]{3,1,2,0:T(2,128)(2,1)S(1)}, bf16[2,2,12,4096]{3,1,2,0:T(2,128)(2,1)S(1)}, u32[]{:S(2)}, u32[]{:S(2)}) %collective-permute-start.1) | collective-permute-done | bytes 393248 | tf_op jit(solution)/shard_map/ppermute | solution.py:52
  201.3 8.9 %collective-permute-done = bf16[2,2,12,4096]{3,1,2,0:T(2,128)(2,1)S(1)} collective-permute-done((bf16[2,2,12,4096]{3,1,2,0:T(2,128)(2,1)S(1)}, bf16[2,2,12,4096]{3,1,2,0:T(2,128)(2,1)S(1)}, u32[]{:S(2)}, u32[]{:S(2)}) %collective-permute-start) | collective-permute-done | bytes 393248 | tf_op jit(solution)/shard_map/ppermute | solution.py:52
  210.2 1.1 pad_maximum_fusion
  211.4 2.1 gather_fusion.1
  213.5 0.7 fusion.16
  214.2 0.8 copy.27
  215.0 1.0 reshape_reshape.11
  216.1 1.1 fusion.5
  217.2 0.3 copy-done.3
  217.5 2.7 %fusion.3 = f32[4,2,12,64,64]{3,4,0,1,2:T(8,128)} fusion(f32[2,4,64,64,12]{3,4,2,1,0:T(8,128)S(1)} %fusion.5, bf16[4,2,12,64,64]{3,4,0,1,2:T(8,128)(2,1)S(1)} %copy-done.3, f32[12]{0:T(128)S(1)} %compare_convert_fusion), kind=kLoop, calls=%fused_computation.7 | loop fusion | flops 1179648 | bytes 3932208 | tf_op jit(solution)/shard_map/mul | solution.py:71
  220.2 3.7 %copy.30 = f32[4,2,12,64,64]{4,3,1,2,0:T(8,128)} copy(f32[4,2,12,64,64]{3,4,0,1,2:T(8,128)} %fusion.3) | data formatting | bytes 3145728 | tf_op jit(solution)/shard_map/mul | solution.py:71
  223.9 4.2 %reshape.105 = f32[4,2,12,4096]{3,1,2,0:T(2,128)} reshape(f32[4,2,12,64,64]{4,3,1,2,0:T(8,128)} %copy.30) | data formatting | bytes 3145728 | tf_op jit(solution)/shard_map/reshape | solution.py:72
  (17 shorter events, 0.1 us)
Async XLA Ops:
  6.5 3.7 %copy-start = (bf16[4,2,47,4096]{3,1,2,0:T(2,128)(2,1)S(1)}, bf16[4,2,47,4096]{3,1,2,0:T(2,128)(2,1)}, u32[]{:S(2)}) copy-start(bf16[4,2,47,4096]{3,1,2,0:T(2,128)(2,1)} %param.5) | copy-start | bytes 9240580
  6.5 105.2 %all-gather.2.cloned.1.call-start = ((), (), s32[]{:S(2)}) async-start(), calls=%async_computation.1 | async-start | bytes 7077888 | tf_op jit(solution)/shard_map/all_gather | solution.py:34
  25.4 5.0 %copy-start.4 = (s32[4]{0:T(128)S(1)}, s32[4]{0:T(128)}, u32[]{:S(2)}) copy-start(s32[4]{0:T(128)} %param.7) | copy-start | bytes 52
  25.4 75.3 %all-to-all-start = ((bf16[4,2,4,12,4096]{4,1,3,0,2:T(2,128)(2,1)}), bf16[4,2,4,12,4096]{4,1,3,0,2:T(2,128)(2,1)}, u32[]{:S(2)}, u32[]{:S(2)}) async-start(bf16[4,2,4,12,4096]{4,1,3,0,2:T(2,128)(2,1)} %broadcast_select_fusion), calls=%async_computation | async-start | bytes 6291456 | tf_op jit(solution)/shard_map/all_to_all | solution.py:32
  150.1 5.6 %copy-start.2 = (bf16[4,2,12,64,64]{3,4,0,1,2:T(8,128)(2,1)}, bf16[4,2,12,64,64]{3,4,0,1,2:T(8,128)(2,1)S(1)}, u32[]{:S(2)}) copy-start(bf16[4,2,12,64,64]{3,4,0,1,2:T(8,128)(2,1)S(1)} %fusion.11) | copy-start | bytes 2359300
  155.7 45.6 %collective-permute-start.1 = (bf16[2,2,12,4096]{3,1,2,0:T(2,128)(2,1)S(1)}, bf16[2,2,12,4096]{3,1,2,0:T(2,128)(2,1)S(1)}, u32[]{:S(2)}, u32[]{:S(2)}) collective-permute-start(bf16[2,2,12,4096]{3,1,2,0:T(2,128)(2,1)S(1)} %get-tuple-element.6), channel_id=1, source_target_pairs={{0,1},{1,0},{2,9},{3,8},{4,17},{5,16},{6,25},{7,24},{8,3},{9,2},{1... | collective-permute-start | bytes 1179656 | tf_op jit(solution)/shard_map/ppermute | solution.py:52
  155.8 54.4 %collective-permute-start = (bf16[2,2,12,4096]{3,1,2,0:T(2,128)(2,1)S(1)}, bf16[2,2,12,4096]{3,1,2,0:T(2,128)(2,1)S(1)}, u32[]{:S(2)}, u32[]{:S(2)}) collective-permute-start(bf16[2,2,12,4096]{3,1,2,0:T(2,128)(2,1)S(1)} %get-tuple-element.5), channel_id=1, source_target_pairs={{0,0},{1,1},{2,8},{3,9},{4,16},{5,17},{6,24},{7,25},{8,2},{9,3},{1... | collective-permute-start | bytes 1179656 | tf_op jit(solution)/shard_map/ppermute | solution.py:52
  216.1 1.4 copy-start.3
  220.2 7.9 %copy-start.1 = (bf16[4,2,47,4096]{3,1,2,0:T(2,128)(2,1)S(1)}, bf16[4,2,47,4096]{3,1,2,0:T(2,128)(2,1)}, u32[]{:S(2)}) copy-start(bf16[4,2,47,4096]{3,1,2,0:T(2,128)(2,1)} %param.5) | copy-start | bytes 9240580
Sparse Core Ops, SparseCore 0:
  9.5 47.0 all-gather.1
where the time goes:
time: 236 us; the launch traced here: 235 us
  waiting for transfers between devices  118 us (50%)
  local copies, waits for them, and re-layouts  68.9 us (29%)
  between operations  13.6 us (6%)
  matrix products  12.2 us (5%)
  other arithmetic  11.9 us (5%)
  starting transfers between devices  10.9 us (5%)
    all_to_all x1, waiting for transfers between devices, on_device(): lax.all_to_all(packed, 'row', split_axis=2, concat_axis=0, tiled=True)  69 us
    ppermute x2, waiting for transfers between devices, on_device(): lax.ppermute(block, ('row', 'col'), mirror_pairs(row_devices, col_devices...  48.5 us
    reshape x1, local copies, waits for them, and re-layouts, on_device(): piece.reshape(occ_row, piece_count, slot_count, tile_width, tile_width)  17.9 us
    another operation x1, local copies, waits for them, and re-layouts, on_device(): received.reshape(piece_count, occ_col, slot_count, tile_width, tile_width)  11.1 us
    dot_general x1, matrix products, on_device(): jnp.einsum('iksac,kjscb->ijsab', left_tiles, right_tiles, preferred_eleme...  11.1 us
    all_gather x1, local copies, waits for them, and re-layouts, on_device(): piece = lax.all_gather(amplitudes, 'col', axis=1, tiled=True)  9.34 us
    gather x1, local copies, waits for them, and re-layouts, on_device(): packed = jnp.take(integrals, tile_second.reshape(-1), axis=2)  8.51 us
    select_n x2, other arithmetic, on_device(): packed = jnp.take(integrals, tile_second.reshape(-1), axis=2)  6.63 us
  transfers between devices with their start and end apart: 4, of which 3 were waited for; matrix products, arithmetic and copies ran while one was open for 12% of the time, Pallas kernels for 0%

commit v1 on v0

--- a/solution.py
+++ b/solution.py
@@ -4,6 +4,20 @@
 from jax.sharding import PartitionSpec as P
 
 TILE = 64
+
+
+def stocks_move(a0, d0, matrix):
+    new, o_now = (a0.shape[:d0], a0.shape[d0 + 1 :])
+    found_now = a0.reshape(*new, matrix, -1, *o_now)
+    return jnp.moveaxis(found_now, d0, 0)
+
+
+def map_the_sources_all(w_in, axis_k):
+    w_in = jnp.moveaxis(w_in, 0, axis_k)
+    all_rows = w_in.shape
+    return w_in.reshape(
+        *all_rows[:axis_k], all_rows[axis_k] * all_rows[axis_k + 1], *all_rows[axis_k + 2 :]
+    )
 
 
 def mirror_pairs(row_devices, col_devices, step):
@@ -29,7 +43,19 @@
     tile_second = pair_lists[:, :, 1]
     packed = jnp.take(integrals, tile_second.reshape(-1), axis=2)
     packed = packed.reshape(occ_row, occ_col, row_devices, slot_count, square)
-    received = lax.all_to_all(packed, "row", split_axis=2, concat_axis=0, tiled=True)
+    val = lax.axis_size("row")
+    piece_now = lax.axis_index("row")
+    state_now, f_next = (val, piece_now)
+    raw_out = stocks_move(packed, 2, state_now)
+    queue = [raw_out[f_next]]
+    for dev_i in range(1, state_now):
+        r2 = raw_out[(f_next + dev_i) % state_now]
+        aux = lax.ppermute(
+            r2, axis_name="row", perm=[(pp, (pp + dev_i) % state_now) for pp in range(state_now)]
+        )
+        queue.append(aux)
+    raw_out = jnp.stack(queue, 0)[(f_next - jnp.arange(state_now)) % state_now]
+    received = map_the_sources_all(raw_out, 0)
     received = received.reshape(occ_row * row_devices, occ_col, slot_count, square)
     piece = lax.all_gather(amplitudes, "col", axis=1, tiled=True)
     piece_count = piece.shape[1]

time: 236 us -> 252 us (1.068)
  local copies, waits for them, and re-layouts: 68.9 us -> 85 us
  other arithmetic: 11.9 us -> 16.7 us
  waiting for transfers between devices: 118 us -> 114 us
    all_to_all x1 -> x0, waiting for transfers between devices: 69 us -> none  [on_device(): lax.all_to_all(packed, 'row', split_axis=2, concat_axis=0, tiled=True)]
    ppermute x0 -> x3, waiting for transfers between devices: none -> 65.3 us  [on_device(): lax.ppermute(r2, axis_name='row', perm=[(pp, (pp + dev_i) % state_now) fo...]
    gather x0 -> x2, local copies, waits for them, and re-layouts: none -> 13.5 us  [on_device(): raw_out = jnp.stack(queue, 0)[(f_next - jnp.arange(state_now)) % state_now]]
    another operation x0 -> x1, other arithmetic: none -> 5.08 us  [on_device(): raw_out = jnp.stack(queue, 0)[(f_next - jnp.arange(state_now)) % state_now]]
    all_to_all x1 -> x0, starting transfers between devices: 4.97 us -> none  [on_device(): lax.all_to_all(packed, 'row', split_axis=2, concat_axis=0, tiled=True)]
    ppermute x0 -> x3, starting transfers between devices: none -> 3.79 us  [on_device(): lax.ppermute(r2, axis_name='row', perm=[(pp, (pp + dev_i) % state_now) fo...]
    dynamic_slice x0 -> x1, local copies, waits for them, and re-layouts: none -> 2.58 us  [on_device(): queue = [raw_out[f_next]]]
  transfers between devices with their start and end apart: 4 -> 6, of which waited for: 3 -> 4; matrix products, arithmetic and copies ran while one was open for 12% -> 20% of each run, Pallas kernels for 0% -> 0%
where the time goes in v1:
time: 252 us; the launch traced here: 251 us
  waiting for transfers between devices  114 us (45%)
  local copies, waits for them, and re-layouts  85 us (34%)
  other arithmetic  16.7 us (7%)
  between operations  13.6 us (5%)
  matrix products  12.2 us (5%)
  starting transfers between devices  9.77 us (4%)
    ppermute x3, waiting for transfers between devices, on_device(): lax.ppermute(r2, axis_name='row', perm=[(pp, (pp + dev_i) % state_now) fo...  65.3 us
    ppermute x2, waiting for transfers between devices, on_device(): lax.ppermute(block, ('row', 'col'), mirror_pairs(row_devices, col_devices...  48.5 us
    reshape x1, local copies, waits for them, and re-layouts, on_device(): piece.reshape(occ_row, piece_count, slot_count, tile_width, tile_width)  17.9 us
    gather x2, local copies, waits for them, and re-layouts, on_device(): raw_out = jnp.stack(queue, 0)[(f_next - jnp.arange(state_now)) % state_now]  13.5 us
    another operation x1, local copies, waits for them, and re-layouts, on_device(): received.reshape(piece_count, occ_col, slot_count, tile_width, tile_width)  11.1 us
    dot_general x1, matrix products, on_device(): jnp.einsum('iksac,kjscb->ijsab', left_tiles, right_tiles, preferred_eleme...  11.1 us
    all_gather x1, local copies, waits for them, and re-layouts, on_device(): piece = lax.all_gather(amplitudes, 'col', axis=1, tiled=True)  9.35 us
    gather x1, local copies, waits for them, and re-layouts, on_device(): packed = jnp.take(integrals, tile_second.reshape(-1), axis=2)  8.51 us
  transfers between devices with their start and end apart: 6, of which 4 were waited for; matrix products, arithmetic and copies ran while one was open for 20% of the time, Pallas kernels for 0%

profile of v1, /device:TPU:3, one launch (start us, length us, event | category | flops | bytes accessed | tf_op | source)
XLA Modules:
  0.0 251.0 jit_solution(12822080569534361195)
XLA Ops:
  6.5 2.8 %copy.24 = bf16[4,2,12,4096]{3,0,2,1:T(4,128)(2,1)} copy(bf16[4,2,12,4096]{3,1,2,0:T(2,128)(2,1)} %param.4) | data formatting | bytes 1572864 | tf_op args[0]
  9.4 0.8 fusion.35
  10.3 8.5 %gather_fusion = bf16[48,4,2,4096]{3,2,1,0:T(2,128)(2,1)} fusion(bf16[4,2,47,4096]{3,1,2,0:T(2,128)(2,1)S(1)} %copy-done, s32[1024]{0:T(1024)S(1)} %pad_clamp_fusion.2), kind=kCustom, calls=%fused_computation | custom fusion | bytes 6291648 | tf_op jit(solution)/shard_map/jit(_take)/gather | solution.py:44
  18.8 6.4 %copy_select_fusion = bf16[4,2,4,1,12,4096]{5,0,4,1,3,2:T(4,128)(2,1)S(1)} fusion(bf16[4,2,4,1,12,4096]{5,1,0,4,2,3:T(2,128)(2,1)} %bitcast.85, pred[4,12]{1,0:T(4,128)(4,1)S(1)} %compare_and_fusion.1), kind=kLoop, calls=%fused_computation.11 | loop fusion | flops 1572864 | bytes 6291504 | tf_op jit(solution)/shard_map/jit(_take)/select_n | solution.py:44
  25.2 2.6 %dynamic-slice_bitcast_fusion.3 = (bf16[1,4,2,1,12,4096]{5,1,4,2,0,3:T(4,128)(2,1)S(1)}, bf16[4,2,1,12,4096]{4,0,3,1,2:T(4,128)(2,1)}, bf16[4,2,1,12,4096]{4,0,3,1,2:T(4,128)(2,1)}, bf16[4,2,1,12,4096]{4,0,3,1,2:T(4,128)(2,1)}) fusion(bf16[4,2,4,1,12,4096]{5,0,4,1,3,2:T(4,128)(2,1)S(1)} %copy_select_fusion, s32[]{:T(128)S(6)} %select_n.125, ...), kind=kLoop, calls=%fused_computation.20 | loop fusion | bytes 6291472 | tf_op jit(solution)/shard_map/dynamic_slice | solution.py:50
  27.8 3.3 %collective-permute-start.2 = (bf16[4,2,1,12,4096]{4,0,3,1,2:T(4,128)(2,1)}, bf16[4,2,1,12,4096]{4,0,3,1,2:T(4,128)(2,1)S(1)}, u32[]{:S(2)}, u32[]{:S(2)}) collective-permute-start(bf16[4,2,1,12,4096]{4,0,3,1,2:T(4,128)(2,1)} %get-tuple-element.6), channel_id=1, source_target_pairs={{0,24},{8,0},{16,8},{24,16},{1,25},{9,1},{17,9},{25,17},{2,26},{10... | collective-permute-start | bytes 2359304 | tf_op jit(solution)/shard_map/ppermute | solution.py:53
  31.6 0.6 dynamic_slice.31
  32.7 15.1 %collective-permute-done.2 = bf16[4,2,1,12,4096]{4,0,3,1,2:T(4,128)(2,1)S(1)} collective-permute-done((bf16[4,2,1,12,4096]{4,0,3,1,2:T(4,128)(2,1)}, bf16[4,2,1,12,4096]{4,0,3,1,2:T(4,128)(2,1)S(1)}, u32[]{:S(2)}, u32[]{:S(2)}) %collective-permute-start.2) | collective-permute-done | bytes 786464 | tf_op jit(solution)/shard_map/ppermute | solution.py:53
  47.9 50.2 %collective-permute-done.1 = bf16[4,2,1,12,4096]{4,0,3,1,2:T(4,128)(2,1)S(1)} collective-permute-done((bf16[4,2,1,12,4096]{4,0,3,1,2:T(4,128)(2,1)}, bf16[4,2,1,12,4096]{4,0,3,1,2:T(4,128)(2,1)S(1)}, u32[]{:S(2)}, u32[]{:S(2)}) %collective-permute-start.1) | collective-permute-done | bytes 786464 | tf_op jit(solution)/shard_map/ppermute | solution.py:53
  98.1 5.1 %maximum_bitcast_fusion = bf16[4,4,2,12,4096]{4,1,3,2,0:T(4,128)(2,1)} fusion(bf16[1,4,2,1,12,4096]{5,1,4,2,0,3:T(4,128)(2,1)S(1)} %bitcast.86, bf16[1,4,2,1,12,4096]{5,1,4,2,0,3:T(4,128)(2,1)S(1)} %bitcast.87, bf16[1,4,2,1,12,4096]{5,1,4,2,0,3:T(4,128)(2,1)} %bitcast.6, bf16[1,4,2,1,12,4096]{5,1,4,2,0,3:T(4,128)(2,1)S(1)} %get-tuple-element.5), kind=kLoop, calls=%fused_computation.6 | loop fusion | flops 4718592 | bytes 6291456 | tf_op jit(solution)/shard_map/stack | solution.py:57
  103.2 6.6 %gather_fusion.1 = bf16[4,4,2,12,4096]{4,1,3,2,0:T(4,128)(2,1)} fusion(bf16[4,4,2,12,4096]{4,1,3,2,0:T(4,128)(2,1)} %maximum_bitcast_fusion, s32[1024]{0:T(1024)S(1)} %pad_clamp_fusion.1), kind=kCustom, calls=%fused_computation.1 | custom fusion | bytes 6291472 | tf_op jit(solution)/shard_map/gather | solution.py:57
  109.8 6.9 %copy.23 = bf16[4,4,2,12,4096]{4,2,3,1,0:T(2,128)(2,1)} copy(bf16[4,4,2,12,4096]{4,1,3,2,0:T(4,128)(2,1)} %gather_fusion.1) | data formatting | bytes 6291456 | tf_op jit(solution)/shard_map/gather | solution.py:57
  116.7 11.1 %reshape_reshape_reshape.3 = bf16[16,2,12,64,64]{4,3,1,2,0:T(8,128)(2,1)} reshape(bf16[4,4,2,12,4096]{4,2,3,1,0:T(2,128)(2,1)} %copy.23) | data formatting | bytes 6291456 | tf_op jit(solution)/shard_map/reshape;reshape;reshape | solution.py:63
  127.8 9.4 %copy.25 = bf16[4,16,12,4096]{3,1,0,2:T(8,128)(2,1)} copy(bf16[4,16,12,4096]{3,0,2,1:T(4,128)(2,1)} %all-gather.2.cloned.1.call-done) | data formatting | bytes 12582912 | tf_op jit(solution)/shard_map/all_gather | solution.py:60
  137.1 17.9 %reshape.199 = bf16[4,16,12,64,64,1]{4,3,1,0,2,5:T(8,128)(2,1)} reshape(bf16[4,16,12,4096]{3,1,0,2:T(8,128)(2,1)} %copy.25) | data formatting | bytes 12582912 | tf_op jit(solution)/shard_map/reshape | solution.py:62
  155.0 11.1 %fusion.11 = bf16[4,2,12,64,64]{3,4,0,1,2:T(8,128)(2,1)S(1)} fusion(f32[12]{0:T(128)S(1)} %compare_convert_fusion, bf16[4,16,12,64,64,1]{4,3,1,0,2,5:T(8,128)(2,1)} %reshape.199, bf16[16,2,12,64,64]{4,3,1,2,0:T(8,128)(2,1)} %reshape_reshape_reshape.3), kind=kOutput, calls=%fused_computation.15 | convolution fusion | flops 806092800 | bytes 10223664 | tf_op jit(solution)/shard_map/iksac,kjscb->ijsab/dot_general | solution.py:64
  166.2 1.7 copy.27
  167.9 3.1 %reshape_reshape.7 = bf16[2,2,2,12,4096]{4,2,3,1,0:T(2,128)(2,1)S(1)} reshape(bf16[4,2,12,64,64]{4,3,1,2,0:T(8,128)(2,1)} %copy.27) | data formatting | bytes 1572864 | tf_op jit(solution)/shard_map/reshape;reshape | solution.py:71
  170.9 0.8 dynamic-slice_bitcast_fusion.5
  171.8 2.1 collective-permute-start.4
  173.9 3.8 %collective-permute-start.3 = (bf16[2,2,12,4096]{3,1,2,0:T(2,128)(2,1)S(1)}, bf16[2,2,12,4096]{3,1,2,0:T(2,128)(2,1)S(1)}, u32[]{:S(2)}, u32[]{:S(2)}) collective-permute-start(bf16[2,2,12,4096]{3,1,2,0:T(2,128)(2,1)S(1)} %get-tuple-element.9), channel_id=1, source_target_pairs={{0,0},{1,1},{2,8},{3,9},{4,16},{5,17},{6,24},{7,25},{8,2},{9,3},{1... | collective-permute-start | bytes 1179656 | tf_op jit(solution)/shard_map/ppermute | solution.py:78
  177.8 39.5 %collective-permute-done.4 = bf16[2,2,12,4096]{3,1,2,0:T(2,128)(2,1)S(1)} collective-permute-done((bf16[2,2,12,4096]{3,1,2,0:T(2,128)(2,1)S(1)}, bf16[2,2,12,4096]{3,1,2,0:T(2,128)(2,1)S(1)}, u32[]{:S(2)}, u32[]{:S(2)}) %collective-permute-start.4) | collective-permute-done | bytes 393248 | tf_op jit(solution)/shard_map/ppermute | solution.py:78
  217.4 8.9 %collective-permute-done.3 = bf16[2,2,12,4096]{3,1,2,0:T(2,128)(2,1)S(1)} collective-permute-done((bf16[2,2,12,4096]{3,1,2,0:T(2,128)(2,1)S(1)}, bf16[2,2,12,4096]{3,1,2,0:T(2,128)(2,1)S(1)}, u32[]{:S(2)}, u32[]{:S(2)}) %collective-permute-start.3) | collective-permute-done | bytes 393248 | tf_op jit(solution)/shard_map/ppermute | solution.py:78
  226.3 1.1 pad_maximum_fusion
  227.4 2.1 gather_fusion.2
  229.6 0.7 fusion.16
  230.3 0.8 copy.28
  231.1 1.0 reshape_reshape.8
  232.2 1.1 fusion.5
  233.6 2.7 %fusion.3 = f32[4,2,12,64,64]{3,4,0,1,2:T(8,128)} fusion(f32[2,4,64,64,12]{3,4,2,1,0:T(8,128)S(1)} %fusion.5, bf16[4,2,12,64,64]{3,4,0,1,2:T(8,128)(2,1)S(1)} %copy-done.3, f32[12]{0:T(128)S(1)} %compare_convert_fusion), kind=kLoop, calls=%fused_computation.8 | loop fusion | flops 1179648 | bytes 3932208 | tf_op jit(solution)/shard_map/mul | solution.py:97
  236.3 3.7 %copy.31 = f32[4,2,12,64,64]{4,3,1,2,0:T(8,128)} copy(f32[4,2,12,64,64]{3,4,0,1,2:T(8,128)} %fusion.3) | data formatting | bytes 3145728 | tf_op jit(solution)/shard_map/mul | solution.py:97
  240.0 4.2 %reshape.170 = f32[4,2,12,4096]{3,1,2,0:T(2,128)} reshape(f32[4,2,12,64,64]{4,3,1,2,0:T(8,128)} %copy.31) | data formatting | bytes 3145728 | tf_op jit(solution)/shard_map/reshape | solution.py:98
  (27 shorter events, 1.5 us)
Async XLA Ops:
  6.5 3.7 %copy-start = (bf16[4,2,47,4096]{3,1,2,0:T(2,128)(2,1)S(1)}, bf16[4,2,47,4096]{3,1,2,0:T(2,128)(2,1)}, u32[]{:S(2)}) copy-start(bf16[4,2,47,4096]{3,1,2,0:T(2,128)(2,1)} %param.5) | copy-start | bytes 9240580
  6.5 121.2 %all-gather.2.cloned.1.call-start = ((), (), s32[]{:S(2)}) async-start(), calls=%async_computation | async-start | bytes 7077888 | tf_op jit(solution)/shard_map/all_gather | solution.py:60
  25.2 6.4 %copy-start.4 = (s32[4]{0:T(128)S(1)}, s32[4]{0:T(128)}, u32[]{:S(2)}) copy-start(s32[4]{0:T(128)} %param.7) | copy-start | bytes 52
  27.8 20.0 %collective-permute-start.2 = (bf16[4,2,1,12,4096]{4,0,3,1,2:T(4,128)(2,1)}, bf16[4,2,1,12,4096]{4,0,3,1,2:T(4,128)(2,1)S(1)}, u32[]{:S(2)}, u32[]{:S(2)}) collective-permute-start(bf16[4,2,1,12,4096]{4,0,3,1,2:T(4,128)(2,1)} %get-tuple-element.6), channel_id=1, source_target_pairs={{0,24},{8,0},{16,8},{24,16},{1,25},{9,1},{17,9},{25,17},{2,26},{10... | collective-permute-start | bytes 2359304 | tf_op jit(solution)/shard_map/ppermute | solution.py:53
  31.1 66.9 %collective-permute-start.1 = (bf16[4,2,1,12,4096]{4,0,3,1,2:T(4,128)(2,1)}, bf16[4,2,1,12,4096]{4,0,3,1,2:T(4,128)(2,1)S(1)}, u32[]{:S(2)}, u32[]{:S(2)}) collective-permute-start(bf16[4,2,1,12,4096]{4,0,3,1,2:T(4,128)(2,1)} %get-tuple-element.7), channel_id=1, source_target_pairs={{0,16},{8,24},{16,0},{24,8},{1,17},{9,25},{17,1},{25,9},{2,18},{10... | collective-permute-start | bytes 2359304 | tf_op jit(solution)/shard_map/ppermute | solution.py:53
  31.1 66.9 %collective-permute-start = (bf16[4,2,1,12,4096]{4,0,3,1,2:T(4,128)(2,1)}, bf16[4,2,1,12,4096]{4,0,3,1,2:T(4,128)(2,1)}, u32[]{:S(2)}, u32[]{:S(2)}) collective-permute-start(bf16[4,2,1,12,4096]{4,0,3,1,2:T(4,128)(2,1)} %get-tuple-element.8), channel_id=1, source_target_pairs={{0,8},{8,16},{16,24},{24,0},{1,9},{9,17},{17,25},{25,1},{2,10},{10... | collective-permute-start | bytes 2359304 | tf_op jit(solution)/shard_map/ppermute | solution.py:53
  166.1 5.6 %copy-start.2 = (bf16[4,2,12,64,64]{3,4,0,1,2:T(8,128)(2,1)}, bf16[4,2,12,64,64]{3,4,0,1,2:T(8,128)(2,1)S(1)}, u32[]{:S(2)}) copy-start(bf16[4,2,12,64,64]{3,4,0,1,2:T(8,128)(2,1)S(1)} %fusion.11) | copy-start | bytes 2359300
  171.8 45.6 %collective-permute-start.4 = (bf16[2,2,12,4096]{3,1,2,0:T(2,128)(2,1)S(1)}, bf16[2,2,12,4096]{3,1,2,0:T(2,128)(2,1)S(1)}, u32[]{:S(2)}, u32[]{:S(2)}) collective-permute-start(bf16[2,2,12,4096]{3,1,2,0:T(2,128)(2,1)S(1)} %get-tuple-element.10), channel_id=1, source_target_pairs={{0,1},{1,0},{2,9},{3,8},{4,17},{5,16},{6,25},{7,24},{8,3},{9,2},{1... | collective-permute-start | bytes 1179656 | tf_op jit(solution)/shard_map/ppermute | solution.py:78
  173.9 52.4 %collective-permute-start.3 = (bf16[2,2,12,4096]{3,1,2,0:T(2,128)(2,1)S(1)}, bf16[2,2,12,4096]{3,1,2,0:T(2,128)(2,1)S(1)}, u32[]{:S(2)}, u32[]{:S(2)}) collective-permute-start(bf16[2,2,12,4096]{3,1,2,0:T(2,128)(2,1)S(1)} %get-tuple-element.9), channel_id=1, source_target_pairs={{0,0},{1,1},{2,8},{3,9},{4,16},{5,17},{6,24},{7,25},{8,2},{9,3},{1... | collective-permute-start | bytes 1179656 | tf_op jit(solution)/shard_map/ppermute | solution.py:78
  232.1 1.4 copy-start.3
  236.2 7.9 %copy-start.1 = (bf16[4,2,47,4096]{3,1,2,0:T(2,128)(2,1)S(1)}, bf16[4,2,47,4096]{3,1,2,0:T(2,128)(2,1)}, u32[]{:S(2)}) copy-start(bf16[4,2,47,4096]{3,1,2,0:T(2,128)(2,1)} %param.5) | copy-start | bytes 9240580
Sparse Core Ops, SparseCore 0:
  9.5 47.0 all-gather.1
